TPU v7x, 32 devices: a whole 2x2x4 slice. The times are simulated.
32 devices in a mesh: row: 4 (over z), col: 8 (over y, x, core).
Axes of the slice: x: 2, y: 2, z: 4, core: 2. Of those that a mesh axis runs over, the one named last changes fastest.
Arguments:
- points: bfloat16 [2, 8192], P(None, ('row', 'col')), may hold values from 0 to 1
- noise_var: float32 [8192], P(('row', 'col')), may hold values from 0.5 to 2
- district: int32 [8192], P(('row', 'col')), may hold values from 0 to 63, never falling along the last dimension, each value on 1 to 512 neighbouring positions
- solution: float32 [32, 8192], P(None, ('row', 'col')), may hold values from -6 to 6
- residual: float32 [32, 8192], P(None, ('row', 'col')), may hold values from -44 to 44
- direction: float32 [32, 8192], P(None, ('row', 'col')), may hold values from -44 to 44
Outputs:
- new_solution: float32 [32, 8192], P(None, ('row', 'col'))
- new_residual: float32 [32, 8192], P(None, ('row', 'col'))
- new_direction: float32 [32, 8192], P(None, ('row', 'col'))
Inputs may be any that keep to these rules, and one draw needn't show every extreme that they name: Samples are ordered by district; every district holds 1 to 512 samples and one holds exactly 512.
All inputs are finite; a program needn't handle non-finite values.
Results may differ from a plain program's by a relative error of at most 0.004.
Values may be sent and summed in bfloat16 or wider, within the bound.
No kernel may reach another device: no remote copies, remote signals or barrier semaphores. Data moves between devices by JAX's collectives and lax.ppermute only.
A program may use at most 64 MiB of HBM per device.

v0:
```python
import math
import jax
import jax.numpy as jnp
from jax import lax
from jax.sharding import PartitionSpec as P

NDIST = 64
root_three = math.sqrt(3.0)
corr_range = 0.05
district_gain = 0.5


def matern_tile(left_points, right_points):
    left_vals = left_points.astype(jnp.float32)
    right_vals = right_points.astype(jnp.float32)
    delta_x = left_vals[0][:, None] - right_vals[0][None, :]
    delta_y = left_vals[1][:, None] - right_vals[1][None, :]
    scaled = root_three / corr_range * jnp.sqrt(delta_x * delta_x + delta_y * delta_y)
    return ((1.0 + scaled) * jnp.exp(-scaled)).astype(jnp.bfloat16)


def small_product(left, right):
    return jnp.dot(left, right, precision=lax.Precision.HIGHEST, preferred_element_type=jnp.float32)


def chol_solve(matrix, rhs_mat):
    factor = jnp.linalg.cholesky(matrix)
    return jax.scipy.linalg.cho_solve((factor, True), rhs_mat)


def per_device(points, noise_var, district, solution, residual, direction):
    local_count = points.shape[1]
    rhs_count = direction.shape[0]
    whole_count = local_count * lax.axis_size("row") * lax.axis_size("col")
    kernel_scale = 1.0 / (corr_range * math.sqrt(whole_count))
    labels = jnp.arange(NDIST, dtype=jnp.int32)
    onehot = (district[None, :] == labels[:, None]).astype(jnp.float32)
    local_sums = small_product(direction, onehot.T)
    local_sizes = jnp.sum(onehot, axis=1)
    local_norm = small_product(residual, residual.T)
    district_sums, sizes = lax.psum((local_sums, local_sizes), ("row", "col"))
    old_norm = lax.psum(local_norm, ("row", "col"))
    lowered = direction.astype(jnp.bfloat16)
    empty = jnp.zeros((rhs_count, local_count), jnp.float32)
    left_points = lax.all_gather(points, ("row", "col"), axis=1, tiled=True)
    left_dir = lax.all_gather(lowered, ("row", "col"), axis=1, tiled=True)
    width_now = left_points.shape[1]
    block_len = 8192

    def one_step(index_now, acc):
        part_points = lax.dynamic_slice_in_dim(left_points, index_now * block_len, block_len, 1)
        part_dir = lax.dynamic_slice_in_dim(left_dir, index_now * block_len, block_len, 1)
        return acc + jnp.dot(
            part_dir, matern_tile(part_points, points), preferred_element_type=jnp.float32
        )

    kernel_part = lax.fori_loop(0, width_now // block_len, one_step, empty)
    weights = district_sums / jnp.sqrt(sizes)[None, :]
    district_part = small_product(weights, onehot)
    image = (
        noise_var[None, :] * direction + kernel_part * kernel_scale + district_gain * district_part
    )
    local_curv = small_product(direction, image.T)
    curvature = lax.psum(local_curv, ("row", "col"))
    alpha = chol_solve(curvature, old_norm)
    new_solution = solution + small_product(alpha.T, direction)
    new_residual = residual - small_product(alpha.T, image)
    new_norm = lax.psum(small_product(new_residual, new_residual.T), ("row", "col"))
    beta = chol_solve(old_norm, new_norm)
    new_direction = new_residual + small_product(beta.T, direction)
    return (new_solution, new_residual, new_direction)


def solution(mesh):
    in_specs = (
        P(None, ("row", "col")),
        P(("row", "col")),
        P(("row", "col")),
        P(None, ("row", "col")),
        P(None, ("row", "col")),
        P(None, ("row", "col")),
    )
    out_specs = (P(None, ("row", "col")), P(None, ("row", "col")), P(None, ("row", "col")))
    return jax.shard_map(
        per_device, mesh=mesh, in_specs=in_specs, out_specs=out_specs, check_vma=False
    )
```

profile of v0, /device:TPU:14, one launch (start us, length us, event | category | flops | bytes accessed | tf_op | source)
XLA Modules:
  0.0 224.8 jit_solution(12056123770513564116)
XLA Ops:
  0.7 29.1 %all_gather.6 = bf16[2,8192]{1,0:T(2,128)(2,1)S(1)} all-gather(bf16[2,256]{1,0:T(2,128)(2,1)} %param.9), channel_id=1, replica_groups=mesh['row'=4,'col'=8] {'row','col'}, dimensions={1}, use_global_device_ids=true | all-gather | bytes 33792 | tf_op jit(solution)/shard_map/all_gather | solution.py:45
  29.8 0.8 fusion.24
  30.5 0.8 convert_element_type.21
  31.3 41.2 %all_gather.7 = bf16[32,8192]{1,0:T(8,128)(2,1)S(1)} all-gather(bf16[32,256]{1,0:T(8,128)(2,1)S(1)} %convert_element_type.21), channel_id=1, replica_groups=mesh['row'=4,'col'=8] {'row','col'}, dimensions={1}, use_global_device_ids=true | all-gather | bytes 540672 | tf_op jit(solution)/shard_map/all_gather | solution.py:46
  72.5 5.2 %fusion.4 = f32[32,256]{1,0:T(8,128)S(1)} fusion(bf16[32,8192]{1,0:T(8,128)(2,1)S(1)} %all_gather.7, f32[256]{0:T(256)S(1)} %bitcast.55, f32[8192]{0:T(1024)S(1)} %bitcast.53, f32[256]{0:T(256)S(1)} %bitcast.54, f32[8192]{0:T(1024)S(1)} %bitcast.52, f32[32,256]{1,0:T(8,128)S(1)} %copy-done, f32[256]{0:T(256)S(1)} %copy-done.5), kind=kOutput, calls=%fused_computation.10 | convolution fusion | flops 155213824 | bytes 658432 | tf_op jit(solution)/shard_map/while/body/eval_jaxpr/dot_general | solution.py:53
  77.7 0.2 convolution_bitcast_fusion
  78.0 49.4 %all-reduce.1 = (f32[32,64]{0,1:T(8,128)S(1)}, f32[64]{0:T(128)S(1)}) all-reduce(f32[32,64]{0,1:T(8,128)S(1)} %convolution_bitcast_fusion, f32[64]{0:T(128)S(1)} %convert_reduce_fusion), channel_id=1, replica_groups=mesh['row'=4,'col'=8] {'row','col'}, use_global_device_ids=true, to_apply=%region_0.0 | all-reduce | flops 2112 | bytes 16896 | tf_op jit(solution)/shard_map/psum | solution.py:41
  127.3 0.3 fusion.1
  127.8 0.2 fusion.25
  128.0 38.5 %all-reduce = (f32[32,32]{0,1:T(8,128)S(1)}, f32[32,32]{0,1:T(8,128)S(1)}) all-reduce(f32[32,32]{0,1:T(8,128)S(1)} %fusion.25, f32[32,32]{0,1:T(8,128)S(1)} %convolution_bitcast_fusion.1), channel_id=1, replica_groups=mesh['row'=4,'col'=8] {'row','col'}, use_global_device_ids=true, to_apply=%region_6.8 | all-reduce | flops 2048 | bytes 16384 | tf_op jit(solution)/shard_map/psum | solution.py:42
  166.6 2.9 %cholesky.55 = f32[32,32]{1,0:T(8,128)S(1)} custom-call(f32[32,32]{1,0:T(8,128)S(1)} %get-tuple-element.31), custom_call_target="Cholesky" | custom-call | tf_op jit(solution)/shard_map/jit(cholesky)/cholesky | solution.py:27
  169.6 0.6 compare_reduce_fusion
  170.2 0.7 fusion.9
  170.9 2.4 %custom-call.9 = f32[1,32,32]{1,2,0:T(8,128)S(1)} custom-call(f32[1,32,32]{2,1,0:T(8,128)S(1)} %fusion.9), custom_call_target="InvertDiagBlocksLowerTriangular" | custom-call | tf_op jit(solution)/shard_map/jit(_cho_solve)/triangular_solve | solution.py:28
  173.3 2.9 %cholesky.44 = f32[32,32]{1,0:T(8,128)S(1)} custom-call(f32[32,32]{1,0:T(8,128)S(1)} %get-tuple-element.32), custom_call_target="Cholesky" | custom-call | tf_op jit(solution)/shard_map/jit(cholesky)/cholesky | solution.py:27
  176.3 0.6 compare_reduce_fusion.1
  176.9 0.7 fusion.8
  177.6 2.4 %custom-call.8 = f32[1,32,32]{1,2,0:T(8,128)S(1)} custom-call(f32[1,32,32]{2,1,0:T(8,128)S(1)} %fusion.8), custom_call_target="InvertDiagBlocksLowerTriangular" | custom-call | tf_op jit(solution)/shard_map/jit(_cho_solve)/triangular_solve | solution.py:28
  180.0 0.2 fusion.17
  180.4 0.2 convolution_subtract_fusion
  180.8 41.9 %psum.39 = f32[32,32]{1,0:T(8,128)S(1)} all-reduce(f32[32,32]{1,0:T(8,128)S(1)} %fusion.26), channel_id=1, replica_groups=mesh['row'=4,'col'=8] {'row','col'}, use_global_device_ids=true, to_apply=%region_7.0 | all-reduce | flops 1024 | bytes 8192 | tf_op jit(solution)/shard_map/psum | solution.py:68
  222.7 0.2 fusion.12
  223.1 0.9 convolution_add_fusion
  223.9 0.8 convolution_add_fusion.1
  (24 shorter events, 1.0 us)
Async XLA Ops:
  0.6 71.8 %copy-start = (f32[32,256]{1,0:T(8,128)S(1)}, f32[32,256]{1,0:T(8,128)}, u32[]{:S(2)}) copy-start(f32[32,256]{1,0:T(8,128)} %param.14) | copy-start | bytes 98308
  0.6 71.8 %copy-start.5 = (f32[256]{0:T(256)S(1)}, f32[256]{0:T(256)}, u32[]{:S(2)}) copy-start(f32[256]{0:T(256)} %param.10) | copy-start | bytes 3076
  72.5 5.2 %copy-start.4 = (s32[256]{0:T(256)S(1)}, s32[256]{0:T(256)}, u32[]{:S(2)}) copy-start(s32[256]{0:T(256)} %param.11) | copy-start | bytes 3076
  72.5 55.3 %copy-start.2 = (f32[32,256]{1,0:T(8,128)S(1)}, f32[32,256]{1,0:T(8,128)}, u32[]{:S(2)}) copy-start(f32[32,256]{1,0:T(8,128)} %param.13) | copy-start | bytes 98308
  127.6 96.3 %copy-start.3 = (f32[32,256]{1,0:T(8,128)S(1)}, f32[32,256]{1,0:T(8,128)}, u32[]{:S(2)}) copy-start(f32[32,256]{1,0:T(8,128)} %param.12) | copy-start | bytes 98308
  180.7 44.1 %copy-start.1 = (f32[32,256]{1,0:T(8,128)}, f32[32,256]{1,0:T(8,128)S(1)}, u32[]{:S(2)}) copy-start(f32[32,256]{1,0:T(8,128)S(1)} %convolution_subtract_fusion) | copy-start | bytes 98308
where the time goes:
time: 225 us
  blocking collectives  200 us (89%)
  other arithmetic  14.3 us (6%)
  matrix products  8.78 us (4%)
    psum x1, blocking collectives, per_device(): district_sums, sizes = lax.psum((local_sums, local_sizes), ('row', 'col'))  49.4 us
    psum x1, blocking collectives, per_device(): lax.psum(small_product(new_residual, new_residual.T), ('row', 'col'))  41.9 us
    all_gather x1, blocking collectives, per_device(): left_dir = lax.all_gather(lowered, ('row', 'col'), axis=1, tiled=True)  41.2 us
    psum x1, blocking collectives, per_device(): old_norm = lax.psum(local_norm, ('row', 'col'))  38.5 us
    all_gather x1, blocking collectives, per_device(): left_points = lax.all_gather(points, ('row', 'col'), axis=1, tiled=True)  29.1 us
    another operation x6, other arithmetic, chol_solve(): factor = jnp.linalg.cholesky(matrix)  7.2 us
    another operation x4, other arithmetic, chol_solve(): return jax.scipy.linalg.cho_solve((factor, True), rhs_mat)  6.17 us
    dot_general x1, matrix products, one_step(): jnp.dot(part_dir, matern_tile(part_points, points), preferred_element_typ...  5.2 us

commit v1 on v0

--- a/solution.py
+++ b/solution.py
@@ -8,6 +8,12 @@
 root_three = math.sqrt(3.0)
 corr_range = 0.05
 district_gain = 0.5
+
+
+def treat_ends_for(mine_x, raw):
+    back = jnp.concatenate([mine_x, raw], 0)
+    current_arr = lax.all_gather(back, axis_name=("row", "col"), axis=1, tiled=True)
+    return jnp.split(current_arr, [mine_x.shape[0]], 0)
 
 
 def matern_tile(left_points, right_points):
@@ -42,8 +48,7 @@
     old_norm = lax.psum(local_norm, ("row", "col"))
     lowered = direction.astype(jnp.bfloat16)
     empty = jnp.zeros((rhs_count, local_count), jnp.float32)
-    left_points = lax.all_gather(points, ("row", "col"), axis=1, tiled=True)
-    left_dir = lax.all_gather(lowered, ("row", "col"), axis=1, tiled=True)
+    left_points, left_dir = treat_ends_for(points, lowered)
     width_now = left_points.shape[1]
     block_len = 8192
 

time: 225 us -> 189 us (0.84)
  blocking collectives: 200 us -> 162 us
    all_gather x2 -> x1, blocking collectives: 70.2 us -> 30.6 us  [treat_ends_for(): lax.all_gather(back, axis_name=('row', 'col'), axis=1, tiled=True)]
where the time goes in v1:
time: 189 us; the launch traced here: 187 us
  blocking collectives  162 us (86%)
  other arithmetic  15 us (8%)
  matrix products  8.89 us (5%)
    psum x1, blocking collectives, per_device(): district_sums, sizes = lax.psum((local_sums, local_sizes), ('row', 'col'))  51.1 us
    psum x1, blocking collectives, per_device(): lax.psum(small_product(new_residual, new_residual.T), ('row', 'col'))  40.6 us
    psum x1, blocking collectives, per_device(): old_norm = lax.psum(local_norm, ('row', 'col'))  39.8 us
    all_gather x1, blocking collectives, treat_ends_for(): lax.all_gather(back, axis_name=('row', 'col'), axis=1, tiled=True)  30.6 us
    another operation x6, other arithmetic, chol_solve(): factor = jnp.linalg.cholesky(matrix)  7.2 us
    another operation x4, other arithmetic, chol_solve(): return jax.scipy.linalg.cho_solve((factor, True), rhs_mat)  6.17 us
    dot_general x1, matrix products, one_step(): jnp.dot(part_dir, matern_tile(part_points, points), preferred_element_typ...  5.32 us

profile of v1, /device:TPU:14, one launch (start us, length us, event | category | flops | bytes accessed | tf_op | source)
XLA Modules:
  0.0 187.0 jit_solution(5370310908700159354)
XLA Ops:
  0.7 0.8 convert_element_type.18
  1.5 0.7 pad_maximum_fusion
  2.2 30.6 %all_gather.3 = bf16[34,8192]{1,0:T(8,128)(2,1)S(1)} all-gather(bf16[34,256]{1,0:T(8,128)(2,1)S(1)} %pad_maximum_fusion), channel_id=1, replica_groups=mesh['row'=4,'col'=8] {'row','col'}, dimensions={1}, use_global_device_ids=true | all-gather | bytes 574464 | tf_op jit(solution)/shard_map/all_gather | solution.py:15
  32.9 5.3 %fusion.3 = f32[32,256]{1,0:T(8,128)S(1)} fusion(f32[256]{0:T(256)S(1)} %bitcast.50, f32[8192]{0:T(1024)S(1)} %bitcast.48, f32[256]{0:T(256)S(1)} %bitcast.49, f32[8192]{0:T(1024)S(1)} %bitcast.47, bf16[34,8192]{1,0:T(8,128)(2,1)S(1)} %all_gather.3, f32[32,256]{1,0:T(8,128)S(1)} %copy-done, f32[256]{0:T(256)S(1)} %copy-done.6), kind=kOutput, calls=%fused_computation.9 | convolution fusion | flops 155213824 | bytes 658432 | tf_op jit(solution)/shard_map/while/body/eval_jaxpr/dot_general | solution.py:58
  38.2 0.2 convolution_bitcast_fusion
  38.5 51.1 %all-reduce.1 = (f32[32,64]{0,1:T(8,128)S(1)}, f32[64]{0:T(128)S(1)}) all-reduce(f32[32,64]{0,1:T(8,128)S(1)} %convolution_bitcast_fusion, f32[64]{0:T(128)S(1)} %convert_reduce_fusion), channel_id=1, replica_groups=mesh['row'=4,'col'=8] {'row','col'}, use_global_device_ids=true, to_apply=%region_0.0 | all-reduce | flops 2112 | bytes 16896 | tf_op jit(solution)/shard_map/psum | solution.py:47
  89.6 0.3 fusion.1
  89.9 0.2 convolution_bitcast_fusion.1
  90.1 0.2 fusion.25
  90.2 39.8 %all-reduce = (f32[32,32]{0,1:T(8,128)S(1)}, f32[32,32]{0,1:T(8,128)S(1)}) all-reduce(f32[32,32]{0,1:T(8,128)S(1)} %fusion.25, f32[32,32]{0,1:T(8,128)S(1)} %convolution_bitcast_fusion.1), channel_id=1, replica_groups=mesh['row'=4,'col'=8] {'row','col'}, use_global_device_ids=true, to_apply=%region_6.8 | all-reduce | flops 2048 | bytes 16384 | tf_op jit(solution)/shard_map/psum | solution.py:48
  130.2 2.9 %cholesky.55 = f32[32,32]{1,0:T(8,128)S(1)} custom-call(f32[32,32]{1,0:T(8,128)S(1)} %get-tuple-element.31), custom_call_target="Cholesky" | custom-call | tf_op jit(solution)/shard_map/jit(cholesky)/cholesky | solution.py:33
  133.2 0.6 compare_reduce_fusion
  133.8 0.7 fusion.9
  134.5 2.4 %custom-call.9 = f32[1,32,32]{1,2,0:T(8,128)S(1)} custom-call(f32[1,32,32]{2,1,0:T(8,128)S(1)} %fusion.9), custom_call_target="InvertDiagBlocksLowerTriangular" | custom-call | tf_op jit(solution)/shard_map/jit(_cho_solve)/triangular_solve | solution.py:34
  136.9 2.9 %cholesky.44 = f32[32,32]{1,0:T(8,128)S(1)} custom-call(f32[32,32]{1,0:T(8,128)S(1)} %get-tuple-element.32), custom_call_target="Cholesky" | custom-call | tf_op jit(solution)/shard_map/jit(cholesky)/cholesky | solution.py:33
  139.9 0.6 compare_reduce_fusion.1
  140.5 0.7 fusion.8
  141.2 2.4 %custom-call.8 = f32[1,32,32]{1,2,0:T(8,128)S(1)} custom-call(f32[1,32,32]{2,1,0:T(8,128)S(1)} %fusion.8), custom_call_target="InvertDiagBlocksLowerTriangular" | custom-call | tf_op jit(solution)/shard_map/jit(_cho_solve)/triangular_solve | solution.py:34
  143.6 0.2 fusion.17
  144.0 0.2 convolution_subtract_fusion
  144.4 40.6 %psum.39 = f32[32,32]{1,0:T(8,128)S(1)} all-reduce(f32[32,32]{1,0:T(8,128)S(1)} %fusion.26), channel_id=1, replica_groups=mesh['row'=4,'col'=8] {'row','col'}, use_global_device_ids=true, to_apply=%region_7.0 | all-reduce | flops 1024 | bytes 8192 | tf_op jit(solution)/shard_map/psum | solution.py:73
  185.0 0.2 fusion.12
  185.3 0.9 convolution_add_fusion
  186.2 0.8 convolution_add_fusion.1
  (27 shorter events, 0.9 us)
Async XLA Ops:
  0.6 32.2 %copy-start = (f32[32,256]{1,0:T(8,128)S(1)}, f32[32,256]{1,0:T(8,128)}, u32[]{:S(2)}) copy-start(f32[32,256]{1,0:T(8,128)} %param.14) | copy-start | bytes 98308
  0.6 32.2 %copy-start.4 = (bf16[2,256]{1,0:T(2,128)(2,1)S(1)}, bf16[2,256]{1,0:T(2,128)(2,1)}, u32[]{:S(2)}) copy-start(bf16[2,256]{1,0:T(2,128)(2,1)} %param.9) | copy-start | bytes 3076
  0.7 32.2 %copy-start.6 = (f32[256]{0:T(256)S(1)}, f32[256]{0:T(256)}, u32[]{:S(2)}) copy-start(f32[256]{0:T(256)} %param.10) | copy-start | bytes 3076
  32.9 5.4 %copy-start.5 = (s32[256]{0:T(256)S(1)}, s32[256]{0:T(256)}, u32[]{:S(2)}) copy-start(s32[256]{0:T(256)} %param.11) | copy-start | bytes 3076
  32.9 57.2 %copy-start.2 = (f32[32,256]{1,0:T(8,128)S(1)}, f32[32,256]{1,0:T(8,128)}, u32[]{:S(2)}) copy-start(f32[32,256]{1,0:T(8,128)} %param.13) | copy-start | bytes 98308
  38.2 148.0 %copy-start.3 = (f32[32,256]{1,0:T(8,128)S(1)}, f32[32,256]{1,0:T(8,128)}, u32[]{:S(2)}) copy-start(f32[32,256]{1,0:T(8,128)} %param.12) | copy-start | bytes 98308
  144.2 42.8 %copy-start.1 = (f32[32,256]{1,0:T(8,128)}, f32[32,256]{1,0:T(8,128)S(1)}, u32[]{:S(2)}) copy-start(f32[32,256]{1,0:T(8,128)S(1)} %convolution_subtract_fusion) | copy-start | bytes 98308
